TPU v7x, 128 devices: a whole 4x4x4 slice. The times are simulated.
128 devices in a mesh: gx: 16 (over z_hi, y, core), gy: 8 (over z_lo, x).
Axes of the slice: x: 4, y: 4, z: 4 (z_hi: 2, z_lo: 2; z = z_hi * 2 + z_lo), core: 2. Of those that a mesh axis runs over, the one named last changes fastest.
Arguments:
- slide_tokens: bfloat16 [128, 1024, 768], P('gy', 'gx'), may hold values from -9 to 9
- tissue: int32 [128, 1024], P('gy', 'gx'), may hold values 0 or 1
- grad_tokens: bfloat16 [128, 1024, 768], P('gy', 'gx'), may hold values from -6 to 6
- w_qkv: bfloat16 [768, 2304], replicated, may hold values from -1 to 1
- w_out: bfloat16 [768, 768], replicated, may hold values from -0.21875 to 0.21875
Outputs:
- block_out: bfloat16 [128, 1024, 768], P('gy', 'gx')
- grad_in: bfloat16 [128, 1024, 768], P('gy', 'gx')
- grad_wqkv: float32 [768, 2304], replicated
- grad_wout: float32 [768, 768], replicated
All inputs are finite; a program needn't handle non-finite values. No bound on the sum of `tissue` on one device may be relied on, other than what follows from the above.
Results may differ from a plain program's by a relative error of at most 0.013.
Values may be sent and summed in bfloat16 or wider, within the bound.
No kernel may reach another device: no remote copies, remote signals or barrier semaphores. Data moves between devices by JAX's collectives and lax.ppermute only.
A program may use at most 256 MiB of HBM per device.

v0:
```python
import math
import jax
import jax.numpy as jnp
from jax import lax
from jax.sharding import PartitionSpec as P

HEADS = 24
WIN = 8
SHIFT = 4
epsilon = 1e-05


def shifted_2(block, axis, distance):
    devices = range(lax.axis_size(axis))
    route = [((i - distance) % len(devices), i) for i in devices]
    return lax.ppermute(block, axis, route)


def windows(tensor):
    row_count, col_count, feature_dim = tensor.shape
    tensor = tensor.reshape(row_count // WIN, WIN, col_count // WIN, WIN, feature_dim)
    return tensor.transpose(0, 2, 1, 3, 4).reshape(-1, WIN * WIN, feature_dim)


def unwindows(tensor, row_count, col_count):
    feature_dim = tensor.shape[-1]
    tensor = tensor.reshape(row_count // WIN, col_count // WIN, WIN, WIN, feature_dim)
    return tensor.transpose(0, 2, 1, 3, 4).reshape(row_count, col_count, feature_dim)


def split_heads(tensor):
    return tensor.reshape(tensor.shape[0], tensor.shape[1], HEADS, -1)


def attend(qkv_win, keep_win):
    model_dim = qkv_win.shape[-1] // 3
    queries = split_heads(qkv_win[..., :model_dim])
    keys_part = split_heads(qkv_win[..., model_dim : 2 * model_dim])
    values_part = split_heads(qkv_win[..., 2 * model_dim :])
    score_scale = 1.0 / math.sqrt(model_dim // HEADS)
    scores = (
        jnp.einsum("wqhd,wkhd->whqk", queries, keys_part, preferred_element_type=jnp.float32)
        * score_scale
    )
    win_tokens = qkv_win.shape[1]
    itself = jnp.eye(win_tokens, dtype=bool)
    allowed = jnp.logical_or(keep_win[:, None, None, :] > 0.5, itself[None, None])
    scores = jnp.where(allowed, scores, -1e30)
    maximum = jnp.max(scores, -1, keepdims=True)
    exponent = jnp.exp(scores - maximum)
    attn_probs = exponent / jnp.sum(exponent, -1, keepdims=True)
    weights_half = attn_probs.astype(jnp.bfloat16)
    mixed_out = jnp.einsum(
        "whqk,wkhd->wqhd", weights_half, values_part, preferred_element_type=jnp.float32
    ).astype(jnp.bfloat16)
    return (mixed_out.reshape(qkv_win.shape[0], win_tokens, model_dim), attn_probs)


def attend_back(qkv_win, attn_probs, grad_mixed):
    model_dim = qkv_win.shape[-1] // 3
    window_count, win_tokens = (qkv_win.shape[0], qkv_win.shape[1])
    queries = split_heads(qkv_win[..., :model_dim])
    keys_part = split_heads(qkv_win[..., model_dim : 2 * model_dim])
    values_part = split_heads(qkv_win[..., 2 * model_dim :])
    score_scale = 1.0 / math.sqrt(model_dim // HEADS)
    grad_heads = split_heads(grad_mixed)
    grad_prob = jnp.einsum(
        "wqhd,wkhd->whqk", grad_heads, values_part, preferred_element_type=jnp.float32
    )
    weights_half = attn_probs.astype(jnp.bfloat16)
    grad_value = jnp.einsum(
        "whqk,wqhd->wkhd", weights_half, grad_heads, preferred_element_type=jnp.float32
    ).astype(jnp.bfloat16)
    grad_score = (
        attn_probs * (grad_prob - jnp.sum(grad_prob * attn_probs, -1, keepdims=True)) * score_scale
    )
    score_half = grad_score.astype(jnp.bfloat16)
    grad_query = jnp.einsum(
        "whqk,wkhd->wqhd", score_half, keys_part, preferred_element_type=jnp.float32
    ).astype(jnp.bfloat16)
    grad_key = jnp.einsum(
        "whqk,wqhd->wkhd", score_half, queries, preferred_element_type=jnp.float32
    ).astype(jnp.bfloat16)
    shape_out = (window_count, win_tokens, model_dim)
    return jnp.concatenate(
        [grad_query.reshape(shape_out), grad_key.reshape(shape_out), grad_value.reshape(shape_out)],
        -1,
    )


def layer_region(shifted, keep_mask, grad_shift, owned_mask, w_qkv, w_out):
    row_count, col_count, model_dim = shifted.shape
    flat_in = shifted.reshape(-1, model_dim).astype(jnp.float32)
    centered = flat_in - jnp.mean(flat_in, -1, keepdims=True)
    inv_sigma = lax.rsqrt(jnp.mean(centered * centered, -1, keepdims=True) + epsilon)
    normed = centered * inv_sigma
    hidden = normed.astype(jnp.bfloat16)
    qkv = jnp.dot(hidden, w_qkv, preferred_element_type=jnp.float32).astype(jnp.bfloat16)
    qkv_win = windows(qkv.reshape(row_count, col_count, -1))
    keep_win = windows(keep_mask[..., None])[..., 0]
    mixed_out, attn_probs = attend(qkv_win, keep_win)
    mixed_flat = unwindows(mixed_out, row_count, col_count).reshape(-1, model_dim)
    output = jnp.dot(mixed_flat, w_out, preferred_element_type=jnp.float32).astype(jnp.bfloat16)
    grad_flat = grad_shift.reshape(-1, model_dim)
    grad_mixed = jnp.dot(grad_flat, w_out.T, preferred_element_type=jnp.float32).astype(
        jnp.bfloat16
    )
    grad_qkv = attend_back(
        qkv_win, attn_probs, windows(grad_mixed.reshape(row_count, col_count, model_dim))
    )
    grad_qkv = unwindows(grad_qkv, row_count, col_count).reshape(-1, 3 * model_dim)
    own_column = owned_mask.reshape(-1, 1).astype(jnp.bfloat16)
    contract = (((0,), (0,)), ((), ()))
    grad_wout = lax.dot_general(
        mixed_flat * own_column, grad_flat, contract, preferred_element_type=jnp.float32
    )
    grad_wqkv = lax.dot_general(
        hidden * own_column, grad_qkv, contract, preferred_element_type=jnp.float32
    )
    grad_hidden = jnp.dot(grad_qkv, w_qkv.T, preferred_element_type=jnp.float32)
    grad_shifted = inv_sigma * (
        grad_hidden
        - jnp.mean(grad_hidden, -1, keepdims=True)
        - normed * jnp.mean(grad_hidden * normed, -1, keepdims=True)
    )
    shape_out = (row_count, col_count, model_dim)
    return (
        output.reshape(shape_out),
        grad_shifted.astype(jnp.bfloat16).reshape(shape_out),
        grad_wqkv,
        grad_wout,
    )


def local(slide_tokens, tissue, grad_tokens, w_qkv, w_out):
    row_count, col_count, model_dim = slide_tokens.shape
    keep_mask = tissue.astype(jnp.bfloat16)
    from_below = shifted_2((slide_tokens[:SHIFT], keep_mask[:SHIFT], grad_tokens[:SHIFT]), "gy", -1)
    tall_x = jnp.concatenate([slide_tokens[SHIFT:], from_below[0]], 0)
    tall_k = jnp.concatenate([keep_mask[SHIFT:], from_below[1]], 0)
    tall_g = jnp.concatenate([grad_tokens[SHIFT:], from_below[2]], 0)
    from_right = shifted_2((tall_x[:, :SHIFT], tall_k[:, :SHIFT], tall_g[:, :SHIFT]), "gx", -1)
    shifted_x = jnp.concatenate([tall_x[:, SHIFT:], from_right[0]], 1)
    shifted_k = jnp.concatenate([tall_k[:, SHIFT:], from_right[1]], 1)
    shifted_g = jnp.concatenate([tall_g[:, SHIFT:], from_right[2]], 1)
    owned_mask = jnp.ones((row_count, col_count), jnp.float32)
    attn_shift, grad_shift, part_qkv, part_out = layer_region(
        shifted_x, shifted_k, shifted_g, owned_mask, w_qkv, w_out
    )
    edge = col_count - SHIFT
    from_left = shifted_2((attn_shift[:, edge:], grad_shift[:, edge:]), "gx", 1)
    wide_attn = jnp.concatenate([from_left[0], attn_shift[:, :edge]], 1)
    wide_grad = jnp.concatenate([from_left[1], grad_shift[:, :edge]], 1)
    bottom = row_count - SHIFT
    from_above = shifted_2((wide_attn[bottom:], wide_grad[bottom:]), "gy", 1)
    attn_tile = jnp.concatenate([from_above[0], wide_attn[:bottom]], 0)
    grad_tile = jnp.concatenate([from_above[1], wide_grad[:bottom]], 0)
    grad_wqkv, grad_wout = lax.psum((part_qkv, part_out), ("gx", "gy"))
    block_out = (slide_tokens.astype(jnp.float32) + attn_tile.astype(jnp.float32)).astype(
        jnp.bfloat16
    )
    grad_in = (grad_tokens.astype(jnp.float32) + grad_tile.astype(jnp.float32)).astype(jnp.bfloat16)
    return (block_out, grad_in, grad_wqkv, grad_wout)


def solution(mesh):
    placed = (P("gy", "gx", None), P("gy", "gx"), P("gy", "gx", None), P(), P())
    return jax.shard_map(
        local,
        mesh=mesh,
        in_specs=placed,
        out_specs=(P("gy", "gx", None), P("gy", "gx", None), P(), P()),
        check_vma=False,
    )
```

profile of v0, /device:TPU:1, one launch (start us, length us, event | category | flops | bytes accessed | tf_op | source)
XLA Modules:
  0.0 433.7 jit_solution(9250790033228147858)
XLA Ops:
  8.1 4.7 %collective-permute-start.2 = (bf16[4,64]{1,0:T(4,128)(2,1)S(1)}, bf16[4,64]{1,0:T(4,128)(2,1)S(1)}, u32[]{:S(2)}, u32[]{:S(2)}) collective-permute-start(bf16[4,64]{1,0:T(4,128)(2,1)S(1)} %slice.99), channel_id=1, source_target_pairs={{1,0},{2,1},{3,2},{4,3},{5,4},{6,5},{7,6},{0,7},{9,8},{10,9},{11,1... | collective-permute-start | bytes 1544 | tf_op jit(solution)/shard_map/ppermute | solution.py:16
  37.5 4.3 collective-permute-start.7
  43.2 2.8 slice_maximum_fusion
  55.5 4.5 %convolution_convert_fusion = bf16[1024,2304]{1,0:T(8,128)(2,1)S(1)} fusion(bf16[1024,768]{1,0:T(8,128)(2,1)S(1)} %fusion.20, bf16[768,2304]{1,0:T(8,128)(2,1)S(1)} %copy-done), kind=kOutput, calls=%fused_computation.12 | convolution fusion | flops 3626237952 | bytes 9830400 | tf_op jit(solution)/shard_map/dot_general | solution.py:98
  62.8 4.1 copy.18
  66.9 4.2 copy.17
  71.1 4.2 copy.15
  75.3 8.2 %reshape_reshape.22 = bf16[16,64,24,32]{3,2,1,0:T(8,128)(2,1)} reshape(bf16[2,8,8,8,768]{4,3,2,1,0:T(8,128)(2,1)} %bitcast.88) | data formatting | bytes 3145728 | tf_op jit(solution)/shard_map/reshape;reshape | solution.py:32
  83.5 7.0 %copy.23 = bf16[16,64,24,32]{1,3,2,0:T(8,128)(2,1)} copy(bf16[16,64,24,32]{3,2,1,0:T(8,128)(2,1)} %reshape_reshape.22) | data formatting | bytes 3145728 | tf_op jit(solution)/shard_map/reshape;reshape | solution.py:32
  90.5 9.2 %fusion.42 = f32[16,24,64,64]{2,3,1,0:T(8,128)} fusion(bf16[16,64,24,32]{1,3,2,0:T(8,128)(2,1)} %copy.23, bf16[16,64,24,32]{1,3,2,0:T(8,128)(2,1)} %bitcast.83), kind=kOutput, calls=%fused_computation.69 | convolution fusion | flops 100663296 | bytes 9437184 | tf_op jit(solution)/shard_map/wqhd,wkhd->whqk/dot_general | solution.py:67
  99.7 10.5 %fusion.41 = (f32[16,24,64]{2,1,0:T(8,128)}, f32[16,24,64,64]{2,3,1,0:T(8,128)}) fusion(pred[16,64,64]{1,2,0:T(8,128)(4,1)} %broadcast_or_fusion, bf16[16,64,24,32]{1,3,2,0:T(8,128)(2,1)} %bitcast.95, bf16[16,64,24,32]{1,3,2,0:T(8,128)(2,1)} %bitcast.93), kind=kOutput, calls=%fused_computation.68 | convolution fusion | flops 106954816 | bytes 9601024 | tf_op jit(solution)/shard_map/sub | solution.py:50
  110.2 19.8 %convert_bitcast_fusion.2 = bf16[16,64,24,32]{1,3,2,0:T(8,128)(2,1)} fusion(bf16[16,64,24,32]{1,3,2,0:T(8,128)(2,1)} %bitcast.94, f32[16,24,64,64]{2,3,1,0:T(8,128)} %fusion.42, f32[16,24,64,64]{2,3,1,0:T(8,128)} %get-tuple-element.12, f32[16,24,64]{2,1,0:T(8,128)} %get-tuple-element.11), kind=kOutput, calls=%fused_computation.24 | convolution fusion | flops 112484416 | bytes 15826944 | tf_op jit(solution)/shard_map/whqk,wkhd->wqhd/dot_general | solution.py:78
  130.0 20.0 %convert_bitcast_fusion.1 = bf16[16,64,24,32]{1,3,2,0:T(8,128)(2,1)} fusion(bf16[16,64,24,32]{1,3,2,0:T(8,128)(2,1)} %bitcast.96, f32[16,24,64,64]{2,3,1,0:T(8,128)} %fusion.42, f32[16,24,64,64]{2,3,1,0:T(8,128)} %get-tuple-element.12, f32[16,24,64]{2,1,0:T(8,128)} %get-tuple-element.11), kind=kOutput, calls=%fused_computation.23 | convolution fusion | flops 112484416 | bytes 15826944 | tf_op jit(solution)/shard_map/whqk,wqhd->wkhd/dot_general | solution.py:81
  150.0 10.7 %convert_bitcast_fusion = bf16[16,64,24,32]{1,3,2,0:T(8,128)(2,1)} fusion(bf16[16,64,24,32]{1,3,2,0:T(8,128)(2,1)} %copy.23, f32[16,24,64,64]{2,3,1,0:T(8,128)} %get-tuple-element.12, f32[16,24,64]{2,1,0:T(8,128)} %get-tuple-element.11), kind=kOutput, calls=%fused_computation.22 | convolution fusion | flops 104595456 | bytes 9535488 | tf_op jit(solution)/shard_map/whqk,wqhd->wkhd/dot_general | solution.py:71
  160.8 8.1 %convert_bitcast_fusion.3 = bf16[16,64,24,32]{1,3,2,0:T(8,128)(2,1)} fusion(bf16[16,64,24,32]{1,3,2,0:T(8,128)(2,1)S(1)} %bitcast.84, f32[16,24,64,64]{2,3,1,0:T(8,128)} %get-tuple-element.12, f32[16,24,64]{2,1,0:T(8,128)S(1)} %copy-done.26), kind=kOutput, calls=%fused_computation.26 | convolution fusion | flops 104595456 | bytes 9535488 | tf_op jit(solution)/shard_map/whqk,wkhd->wqhd/dot_general | solution.py:53
  168.9 6.9 %copy.20 = bf16[16,64,24,32]{3,2,1,0:T(8,128)(2,1)} copy(bf16[16,64,24,32]{1,3,2,0:T(8,128)(2,1)} %convert_bitcast_fusion.3) | data formatting | bytes 3145728 | tf_op jit(solution)/shard_map/convert_element_type | solution.py:55
  175.8 8.2 %reshape_reshape.19 = bf16[2,8,8,8,768]{4,3,2,1,0:T(8,128)(2,1)} reshape(bf16[16,64,24,32]{3,2,1,0:T(8,128)(2,1)} %copy.20) | data formatting | bytes 3145728 | tf_op jit(solution)/shard_map/reshape;reshape | solution.py:27
  186.9 2.9 fusion.44
  189.8 6.9 %copy.30 = bf16[16,64,24,32]{3,2,1,0:T(8,128)(2,1)} copy(bf16[16,64,24,32]{1,3,2,0:T(8,128)(2,1)} %convert_bitcast_fusion) | data formatting | bytes 3145728 | tf_op jit(solution)/shard_map/convert_element_type | solution.py:73
  196.7 8.2 %concatenate.50 = bf16[2,8,8,8,768]{4,3,2,1,0:T(8,128)(2,1)} reshape(bf16[16,64,24,32]{3,2,1,0:T(8,128)(2,1)} %copy.30) | data formatting | bytes 3145728 | tf_op jit(solution)/shard_map/concatenate | solution.py:85
  204.9 6.9 %copy.27 = bf16[16,64,24,32]{3,2,1,0:T(8,128)(2,1)} copy(bf16[16,64,24,32]{1,3,2,0:T(8,128)(2,1)} %convert_bitcast_fusion.1) | data formatting | bytes 3145728 | tf_op jit(solution)/shard_map/convert_element_type | solution.py:83
  211.8 8.2 %concatenate.49 = bf16[2,8,8,8,768]{4,3,2,1,0:T(8,128)(2,1)} reshape(bf16[16,64,24,32]{3,2,1,0:T(8,128)(2,1)} %copy.27) | data formatting | bytes 3145728 | tf_op jit(solution)/shard_map/concatenate | solution.py:85
  220.0 6.9 %copy.25 = bf16[16,64,24,32]{3,2,1,0:T(8,128)(2,1)} copy(bf16[16,64,24,32]{1,3,2,0:T(8,128)(2,1)} %convert_bitcast_fusion.2) | data formatting | bytes 3145728 | tf_op jit(solution)/shard_map/convert_element_type | solution.py:80
  226.9 8.2 %concatenate.48 = bf16[2,8,8,8,768]{4,3,2,1,0:T(8,128)(2,1)} reshape(bf16[16,64,24,32]{3,2,1,0:T(8,128)(2,1)} %copy.25) | data formatting | bytes 3145728 | tf_op jit(solution)/shard_map/concatenate | solution.py:85
  241.2 6.2 %fusion.43 = f32[768,2304]{1,0:T(8,128)} fusion(bf16[1024,768]{1,0:T(8,128)(2,1)S(1)} %bitcast.101, bf16[1024,2304]{1,0:T(8,128)(2,1)S(1)} %bitcast.90), kind=kOutput, calls=%fused_computation.70 | convolution fusion | flops 3623878656 | bytes 13369344 | tf_op jit(solution)/shard_map/dot_general | solution.py:117
  247.5 3.3 convolution_convert_fusion.2
  251.1 4.1 fusion.39
  257.5 6.1 %collective-permute-done.8 = bf16[16,4,768]{2,1,0:T(4,128)(2,1)S(1)} collective-permute-done((bf16[16,4,768]{2,1,0:T(4,128)(2,1)S(1)}, bf16[16,4,768]{2,1,0:T(4,128)(2,1)S(1)}, u32[]{:S(2)}, u32[]{:S(2)}) %collective-permute-start.8) | collective-permute-done | bytes 98336 | tf_op jit(solution)/shard_map/ppermute | solution.py:16
  263.8 3.3 collective-permute-done.5
  269.0 12.7 %collective-permute-done.9 = bf16[4,64,768]{2,1,0:T(8,128)(2,1)S(1)} collective-permute-done((bf16[4,64,768]{2,1,0:T(8,128)(2,1)S(1)}, bf16[4,64,768]{2,1,0:T(8,128)(2,1)S(1)}, u32[]{:S(2)}, u32[]{:S(2)}) %collective-permute-start.9) | collective-permute-done | bytes 393248 | tf_op jit(solution)/shard_map/ppermute | solution.py:16
  283.5 135.1 %all-reduce.3.cloned.1.call-done = (f32[768,2304]{1,0:T(8,128)}, f32[768,768]{1,0:T(8,128)}) async-done(((f32[768,2304]{1,0:T(8,128)}, f32[768,768]{1,0:T(8,128)}), (f32[768,2304]{1,0:T(8,128)}, f32[768,768]{1,0:T(8,128)})) %all-reduce.3.cloned.1.call-update) | async-done | bytes 9437200 | tf_op jit(solution)/shard_map/psum | solution.py:158
  418.6 6.6 %copy.42 = f32[768,2304]{1,0:T(8,128)} copy(f32[768,2304]{1,0:T(8,128)} %get-tuple-element.18) | data formatting | bytes 14155776
  (114 shorter events, 55.9 us)
Async XLA Ops:
  7.2 48.3 %copy-start = (bf16[768,2304]{1,0:T(8,128)(2,1)S(1)}, bf16[768,2304]{1,0:T(8,128)(2,1)}, u32[]{:S(2)}) copy-start(bf16[768,2304]{1,0:T(8,128)(2,1)} %param.8) | copy-start | bytes 10616836
  7.2 411.4 %all-reduce.3.cloned.1.call-start = ((), (), s32[]{:S(2)}) async-start(), calls=%async_computation | async-start | bytes 18874368 | tf_op jit(solution)/shard_map/psum | solution.py:158
  7.2 13.0 %copy-start.9 = (bf16[16,64,768]{2,1,0:T(8,128)(2,1)S(1)}, bf16[16,64,768]{2,1,0:T(8,128)(2,1)}, u32[]{:S(2)}) copy-start(bf16[16,64,768]{2,1,0:T(8,128)(2,1)} %param.7) | copy-start | bytes 4718596
  8.1 13.2 %collective-permute-start.2 = (bf16[4,64]{1,0:T(4,128)(2,1)S(1)}, bf16[4,64]{1,0:T(4,128)(2,1)S(1)}, u32[]{:S(2)}, u32[]{:S(2)}) collective-permute-start(bf16[4,64]{1,0:T(4,128)(2,1)S(1)} %slice.99), channel_id=1, source_target_pairs={{1,0},{2,1},{3,2},{4,3},{5,4},{6,5},{7,6},{0,7},{9,8},{10,9},{11,1... | collective-permute-start | bytes 1544 | tf_op jit(solution)/shard_map/ppermute | solution.py:16
  14.5 21.3 %collective-permute-start.6 = (bf16[4,64,768]{2,1,0:T(8,128)(2,1)}, bf16[4,64,768]{2,1,0:T(8,128)(2,1)}, u32[]{:S(2)}, u32[]{:S(2)}) collective-permute-start(bf16[4,64,768]{2,1,0:T(8,128)(2,1)} %slice.88), channel_id=1, source_target_pairs={{1,0},{2,1},{3,2},{4,3},{5,4},{6,5},{7,6},{0,7},{9,8},{10,9},{11,1... | collective-permute-start | bytes 1179656 | tf_op jit(solution)/shard_map/ppermute | solution.py:16
  16.9 16.0 %collective-permute-start = (bf16[4,64,768]{2,1,0:T(8,128)(2,1)}, bf16[4,64,768]{2,1,0:T(8,128)(2,1)}, u32[]{:S(2)}, u32[]{:S(2)}) collective-permute-start(bf16[4,64,768]{2,1,0:T(8,128)(2,1)} %slice.73), channel_id=1, source_target_pairs={{1,0},{2,1},{3,2},{4,3},{5,4},{6,5},{7,6},{0,7},{9,8},{10,9},{11,1... | collective-permute-start | bytes 1179656 | tf_op jit(solution)/shard_map/ppermute | solution.py:16
  21.3 4.4 %collective-permute-start.3 = (bf16[16,4]{1,0:T(8,128)(2,1)S(1)}, bf16[16,4]{1,0:T(8,128)(2,1)S(1)}, u32[]{:S(2)}, u32[]{:S(2)}) collective-permute-start(bf16[16,4]{1,0:T(8,128)(2,1)S(1)} %pad_maximum_fusion.8), channel_id=1, source_target_pairs={{8,0},{16,8},{24,16},{32,24},{40,32},{48,40},{56,48},{64,56},{72,6... | collective-permute-start | bytes 392 | tf_op jit(solution)/shard_map/ppermute | solution.py:16
  28.6 13.1 %copy-start.7 = (bf16[12,64,768]{2,1,0:T(8,128)(2,1)S(1)}, bf16[12,64,768]{2,1,0:T(8,128)(2,1)}, u32[]{:S(2)}) copy-start(bf16[12,64,768]{2,1,0:T(8,128)(2,1)} %slice.72) | copy-start | bytes 3538948
  30.2 12.9 %copy-start.6 = (bf16[12,64,768]{2,1,0:T(8,128)(2,1)S(1)}, bf16[12,64,768]{2,1,0:T(8,128)(2,1)}, u32[]{:S(2)}) copy-start(bf16[12,64,768]{2,1,0:T(8,128)(2,1)} %slice.87) | copy-start | bytes 3538948
  33.9 12.1 %collective-permute-start.1 = (bf16[16,4,768]{2,1,0:T(4,128)(2,1)S(1)}, bf16[16,4,768]{2,1,0:T(4,128)(2,1)S(1)}, u32[]{:S(2)}, u32[]{:S(2)}) collective-permute-start(bf16[16,4,768]{2,1,0:T(4,128)(2,1)S(1)} %pad_maximum_fusion.7), channel_id=1, source_target_pairs={{8,0},{16,8},{24,16},{32,24},{40,32},{48,40},{56,48},{64,56},{72,6... | collective-permute-start | bytes 294920 | tf_op jit(solution)/shard_map/ppermute | solution.py:16
  37.5 11.2 %collective-permute-start.7 = (bf16[16,4,768]{2,1,0:T(4,128)(2,1)}, bf16[16,4,768]{2,1,0:T(4,128)(2,1)}, u32[]{:S(2)}, u32[]{:S(2)}) collective-permute-start(bf16[16,4,768]{2,1,0:T(4,128)(2,1)} %pad_maximum_fusion.6), channel_id=1, source_target_pairs={{8,0},{16,8},{24,16},{32,24},{40,32},{48,40},{56,48},{64,56},{72,6... | collective-permute-start | bytes 294920 | tf_op jit(solution)/shard_map/ppermute | solution.py:16
  43.2 4.1 copy-start.1
  48.6 2.9 copy-start.25
  53.0 2.0 copy-start.2
  53.0 2.0 copy-start.14
  53.0 2.0 copy-start.21
  150.0 10.8 %copy-start.5 = (bf16[16,64,768]{1,2,0:T(8,128)(2,1)S(1)}, bf16[16,64,768]{1,2,0:T(8,128)(2,1)}, u32[]{:S(2)}) copy-start(bf16[16,64,768]{1,2,0:T(8,128)(2,1)} %copy.15) | copy-start | bytes 4718596
  150.0 10.8 %copy-start.26 = (f32[16,24,64]{2,1,0:T(8,128)S(1)}, f32[16,24,64]{2,1,0:T(8,128)}, u32[]{:S(2)}) copy-start(f32[16,24,64]{2,1,0:T(8,128)} %get-tuple-element.11) | copy-start | bytes 294916
  184.1 2.8 copy-start.19
  239.1 2.2 copy-start.11
  247.5 3.5 copy-start.4
  247.5 3.6 copy-start.12
  247.5 3.6 copy-start.16
  247.5 3.6 copy-start.22
  247.5 3.6 copy-start.24
  250.9 4.4 %collective-permute-start.4 = (bf16[16,4,768]{2,1,0:T(4,128)(2,1)S(1)}, bf16[16,4,768]{2,1,0:T(4,128)(2,1)S(1)}, u32[]{:S(2)}, u32[]{:S(2)}) collective-permute-start(bf16[16,4,768]{2,1,0:T(4,128)(2,1)S(1)} %slice.104), channel_id=1, source_target_pairs={{120,0},{0,8},{8,16},{16,24},{24,32},{32,40},{40,48},{48,56},{56,6... | collective-permute-start | bytes 294920 | tf_op jit(solution)/shard_map/ppermute | solution.py:16
  255.4 11.7 %collective-permute-start.5 = (bf16[4,64,768]{2,1,0:T(8,128)(2,1)S(1)}, bf16[4,64,768]{2,1,0:T(8,128)(2,1)S(1)}, u32[]{:S(2)}, u32[]{:S(2)}) collective-permute-start(bf16[4,64,768]{2,1,0:T(8,128)(2,1)S(1)} %pad_maximum_fusion.5), channel_id=1, source_target_pairs={{7,0},{0,1},{1,2},{2,3},{3,4},{4,5},{5,6},{6,7},{15,8},{8,9},{9,10... | collective-permute-start | bytes 1179656 | tf_op jit(solution)/shard_map/ppermute | solution.py:16
  256.3 10.8 %copy-start.8 = (bf16[16,64,768]{2,1,0:T(8,128)(2,1)S(1)}, bf16[16,64,768]{2,1,0:T(8,128)(2,1)}, u32[]{:S(2)}) copy-start(bf16[16,64,768]{2,1,0:T(8,128)(2,1)} %param.5) | copy-start | bytes 4718596
  257.4 6.2 %collective-permute-start.8 = (bf16[16,4,768]{2,1,0:T(4,128)(2,1)S(1)}, bf16[16,4,768]{2,1,0:T(4,128)(2,1)S(1)}, u32[]{:S(2)}, u32[]{:S(2)}) collective-permute-start(bf16[16,4,768]{2,1,0:T(4,128)(2,1)S(1)} %slice.108), channel_id=1, source_target_pairs={{120,0},{0,8},{8,16},{16,24},{24,32},{32,40},{40,48},{48,56},{56,6... | collective-permute-start | bytes 294920 | tf_op jit(solution)/shard_map/ppermute | solution.py:16
  263.6 18.0 %copy-start.10 = (bf16[16,64,768]{2,1,0:T(8,128)(2,1)S(1)}, bf16[16,64,768]{2,1,0:T(8,128)(2,1)}, u32[]{:S(2)}) copy-start(bf16[16,64,768]{2,1,0:T(8,128)(2,1)} %param.7) | copy-start | bytes 4718596
  263.8 17.9 %collective-permute-start.9 = (bf16[4,64,768]{2,1,0:T(8,128)(2,1)S(1)}, bf16[4,64,768]{2,1,0:T(8,128)(2,1)S(1)}, u32[]{:S(2)}, u32[]{:S(2)}) collective-permute-start(bf16[4,64,768]{2,1,0:T(8,128)(2,1)S(1)} %pad_maximum_fusion.4), channel_id=1, source_target_pairs={{7,0},{0,1},{1,2},{2,3},{3,4},{4,5},{5,6},{6,7},{15,8},{8,9},{9,10... | collective-permute-start | bytes 1179656 | tf_op jit(solution)/shard_map/ppermute | solution.py:16
  418.6 6.6 %copy-start.17 = (f32[768,768]{1,0:T(8,128)S(1)}, f32[768,768]{1,0:T(8,128)}, u32[]{:S(2)}) copy-start(f32[768,768]{1,0:T(8,128)} %get-tuple-element.19) | copy-start | bytes 7077892
  (6 other events, 7.8 us)
Sparse Core Ops, SparseCore 0:
  247.6 170.9 all-reduce.2
where the time goes:
time: 441 us; the launch traced here: 434 us
  waiting for transfers between devices  163 us (37%)
  local copies, waits for them, and re-layouts  119 us (27%)
  matrix products  101 us (23%)
  other arithmetic  21.9 us (5%)
  between operations  14.7 us (3%)
  starting transfers between devices  14.5 us (3%)
    psum x1, waiting for transfers between devices, local(): grad_wqkv, grad_wout = lax.psum((part_qkv, part_out), ('gx', 'gy'))  135 us
    ppermute x10, waiting for transfers between devices, shifted_2(): return lax.ppermute(block, axis, route)  27.6 us
    concatenate x3, local copies, waits for them, and re-layouts, attend_back(): jnp.concatenate([grad_query.reshape(shape_out), grad_key.reshape(shape_ou...  24.6 us
    dot_general x1, matrix products, attend_back(): jnp.einsum('whqk,wqhd->wkhd', score_half, queries, preferred_element_type...  20 us
    dot_general x1, matrix products, attend_back(): jnp.einsum('whqk,wkhd->wqhd', score_half, keys_part, preferred_element_ty...  19.8 us
    another operation x2, local copies, waits for them, and re-layouts, split_heads(): return tensor.reshape(tensor.shape[0], tensor.shape[1], HEADS, -1)  15.2 us
    ppermute x10, starting transfers between devices, shifted_2(): return lax.ppermute(block, axis, route)  14.5 us
    unnamed x56, local copies, waits for them, and re-layouts  14 us
  transfers between devices with their start and end apart: 11, of which 6 were waited for; matrix products, arithmetic and copies ran while one was open for 8% of the time, Pallas kernels for 0%

commit v1 on v0

--- a/solution.py
+++ b/solution.py
@@ -155,7 +155,7 @@
     from_above = shifted_2((wide_attn[bottom:], wide_grad[bottom:]), "gy", 1)
     attn_tile = jnp.concatenate([from_above[0], wide_attn[:bottom]], 0)
     grad_tile = jnp.concatenate([from_above[1], wide_grad[:bottom]], 0)
-    grad_wqkv, grad_wout = lax.psum((part_qkv, part_out), ("gx", "gy"))
+    grad_wqkv, grad_wout = lax.psum(lax.psum((part_qkv, part_out), "gx"), "gy")
     block_out = (slide_tokens.astype(jnp.float32) + attn_tile.astype(jnp.float32)).astype(
         jnp.bfloat16
     )

time: 441 us -> 658 us (1.49)
  waiting for transfers between devices: 163 us -> 376 us
    psum x1 -> x2, waiting for transfers between devices: 135 us -> 345 us  [local(): grad_wqkv, grad_wout = lax.psum(lax.psum((part_qkv, part_out), 'gx'), 'gy')]
    unnamed x56 -> x54, local copies, waits for them, and re-layouts: 14 us -> 13.9 us
  transfers between devices with their start and end apart: 11 -> 12, of which waited for: 6 -> 7; matrix products, arithmetic and copies ran while one was open for 8% -> 6% of each run, Pallas kernels for 0% -> 0%
where the time goes in v1:
time: 658 us; the launch traced here: 651 us
  waiting for transfers between devices  376 us (57%)
  local copies, waits for them, and re-layouts  119 us (18%)
  matrix products  103 us (16%)
  other arithmetic  21.9 us (3%)
  starting transfers between devices  16.1 us (2%)
  between operations  14.7 us (2%)
    psum x2, waiting for transfers between devices, local(): grad_wqkv, grad_wout = lax.psum(lax.psum((part_qkv, part_out), 'gx'), 'gy')  345 us
    ppermute x10, waiting for transfers between devices, shifted_2(): return lax.ppermute(block, axis, route)  31 us
    concatenate x3, local copies, waits for them, and re-layouts, attend_back(): jnp.concatenate([grad_query.reshape(shape_out), grad_key.reshape(shape_ou...  24.6 us
    dot_general x1, matrix products, attend_back(): jnp.einsum('whqk,wqhd->wkhd', score_half, queries, preferred_element_type...  20.1 us
    dot_general x1, matrix products, attend_back(): jnp.einsum('whqk,wkhd->wqhd', score_half, keys_part, preferred_element_ty...  19.8 us
    ppermute x10, starting transfers between devices, shifted_2(): return lax.ppermute(block, axis, route)  16 us
    another operation x2, local copies, waits for them, and re-layouts, split_heads(): return tensor.reshape(tensor.shape[0], tensor.shape[1], HEADS, -1)  15.3 us
    unnamed x54, local copies, waits for them, and re-layouts  13.9 us
  transfers between devices with their start and end apart: 12, of which 7 were waited for; matrix products, arithmetic and copies ran while one was open for 6% of the time, Pallas kernels for 0%

profile of v1, /device:TPU:1, one launch (start us, length us, event | category | flops | bytes accessed | tf_op | source)
XLA Modules:
  0.0 650.6 jit_solution(5361673028761807197)
XLA Ops:
  8.1 4.7 collective-permute-start.2
  37.5 4.3 collective-permute-start.7
  55.5 4.5 convolution_convert_fusion
  62.8 4.2 copy.18
  66.9 4.1 copy.17
  71.1 4.2 copy.15
  75.2 8.2 %reshape_reshape.22 = bf16[16,64,24,32]{3,2,1,0:T(8,128)(2,1)} reshape(bf16[2,8,8,8,768]{4,3,2,1,0:T(8,128)(2,1)} %bitcast.88) | data formatting | bytes 3145728 | tf_op jit(solution)/shard_map/reshape;reshape | solution.py:32
  83.4 7.1 %copy.23 = bf16[16,64,24,32]{1,3,2,0:T(8,128)(2,1)} copy(bf16[16,64,24,32]{3,2,1,0:T(8,128)(2,1)} %reshape_reshape.22) | data formatting | bytes 3145728 | tf_op jit(solution)/shard_map/reshape;reshape | solution.py:32
  90.5 9.2 %fusion.42 = f32[16,24,64,64]{2,3,1,0:T(8,128)} fusion(bf16[16,64,24,32]{1,3,2,0:T(8,128)(2,1)} %copy.23, bf16[16,64,24,32]{1,3,2,0:T(8,128)(2,1)} %bitcast.83), kind=kOutput, calls=%fused_computation.69 | convolution fusion | flops 100663296 | bytes 9437184 | tf_op jit(solution)/shard_map/wqhd,wkhd->whqk/dot_general | solution.py:67
  99.7 10.5 %fusion.41 = (f32[16,24,64]{2,1,0:T(8,128)}, f32[16,24,64,64]{2,3,1,0:T(8,128)}) fusion(pred[16,64,64]{1,2,0:T(8,128)(4,1)} %broadcast_or_fusion, bf16[16,64,24,32]{1,3,2,0:T(8,128)(2,1)} %bitcast.95, bf16[16,64,24,32]{1,3,2,0:T(8,128)(2,1)} %bitcast.93), kind=kOutput, calls=%fused_computation.68 | convolution fusion | flops 106954816 | bytes 9601024 | tf_op jit(solution)/shard_map/sub | solution.py:50
  110.2 19.8 %convert_bitcast_fusion.2 = bf16[16,64,24,32]{1,3,2,0:T(8,128)(2,1)} fusion(bf16[16,64,24,32]{1,3,2,0:T(8,128)(2,1)} %bitcast.94, f32[16,24,64,64]{2,3,1,0:T(8,128)} %fusion.42, f32[16,24,64,64]{2,3,1,0:T(8,128)} %get-tuple-element.14, f32[16,24,64]{2,1,0:T(8,128)} %get-tuple-element.13), kind=kOutput, calls=%fused_computation.24 | convolution fusion | flops 112484416 | bytes 15826944 | tf_op jit(solution)/shard_map/whqk,wkhd->wqhd/dot_general | solution.py:78
  129.9 20.1 %convert_bitcast_fusion.1 = bf16[16,64,24,32]{1,3,2,0:T(8,128)(2,1)} fusion(bf16[16,64,24,32]{1,3,2,0:T(8,128)(2,1)} %bitcast.96, f32[16,24,64,64]{2,3,1,0:T(8,128)} %fusion.42, f32[16,24,64,64]{2,3,1,0:T(8,128)} %get-tuple-element.14, f32[16,24,64]{2,1,0:T(8,128)} %get-tuple-element.13), kind=kOutput, calls=%fused_computation.23 | convolution fusion | flops 112484416 | bytes 15826944 | tf_op jit(solution)/shard_map/whqk,wqhd->wkhd/dot_general | solution.py:81
  150.0 10.7 %convert_bitcast_fusion = bf16[16,64,24,32]{1,3,2,0:T(8,128)(2,1)} fusion(bf16[16,64,24,32]{1,3,2,0:T(8,128)(2,1)} %copy.23, f32[16,24,64,64]{2,3,1,0:T(8,128)} %get-tuple-element.14, f32[16,24,64]{2,1,0:T(8,128)} %get-tuple-element.13), kind=kOutput, calls=%fused_computation.22 | convolution fusion | flops 104595456 | bytes 9535488 | tf_op jit(solution)/shard_map/whqk,wqhd->wkhd/dot_general | solution.py:71
  160.8 8.2 %convert_bitcast_fusion.3 = bf16[16,64,24,32]{1,3,2,0:T(8,128)(2,1)} fusion(bf16[16,64,24,32]{1,3,2,0:T(8,128)(2,1)S(1)} %bitcast.84, f32[16,24,64,64]{2,3,1,0:T(8,128)} %get-tuple-element.14, f32[16,24,64]{2,1,0:T(8,128)S(1)} %copy-done.25), kind=kOutput, calls=%fused_computation.26 | convolution fusion | flops 104595456 | bytes 9535488 | tf_op jit(solution)/shard_map/whqk,wkhd->wqhd/dot_general | solution.py:53
  168.9 6.9 %copy.20 = bf16[16,64,24,32]{3,2,1,0:T(8,128)(2,1)} copy(bf16[16,64,24,32]{1,3,2,0:T(8,128)(2,1)} %convert_bitcast_fusion.3) | data formatting | bytes 3145728 | tf_op jit(solution)/shard_map/convert_element_type | solution.py:55
  175.8 8.2 %reshape_reshape.19 = bf16[2,8,8,8,768]{4,3,2,1,0:T(8,128)(2,1)} reshape(bf16[16,64,24,32]{3,2,1,0:T(8,128)(2,1)} %copy.20) | data formatting | bytes 3145728 | tf_op jit(solution)/shard_map/reshape;reshape | solution.py:27
  186.9 2.9 fusion.44
  189.8 6.9 %copy.30 = bf16[16,64,24,32]{3,2,1,0:T(8,128)(2,1)} copy(bf16[16,64,24,32]{1,3,2,0:T(8,128)(2,1)} %convert_bitcast_fusion) | data formatting | bytes 3145728 | tf_op jit(solution)/shard_map/convert_element_type | solution.py:73
  196.7 8.2 %concatenate.50 = bf16[2,8,8,8,768]{4,3,2,1,0:T(8,128)(2,1)} reshape(bf16[16,64,24,32]{3,2,1,0:T(8,128)(2,1)} %copy.30) | data formatting | bytes 3145728 | tf_op jit(solution)/shard_map/concatenate | solution.py:85
  204.9 6.9 %copy.27 = bf16[16,64,24,32]{3,2,1,0:T(8,128)(2,1)} copy(bf16[16,64,24,32]{1,3,2,0:T(8,128)(2,1)} %convert_bitcast_fusion.1) | data formatting | bytes 3145728 | tf_op jit(solution)/shard_map/convert_element_type | solution.py:83
  211.8 8.2 %concatenate.49 = bf16[2,8,8,8,768]{4,3,2,1,0:T(8,128)(2,1)} reshape(bf16[16,64,24,32]{3,2,1,0:T(8,128)(2,1)} %copy.27) | data formatting | bytes 3145728 | tf_op jit(solution)/shard_map/concatenate | solution.py:85
  220.0 6.9 %copy.25 = bf16[16,64,24,32]{3,2,1,0:T(8,128)(2,1)} copy(bf16[16,64,24,32]{1,3,2,0:T(8,128)(2,1)} %convert_bitcast_fusion.2) | data formatting | bytes 3145728 | tf_op jit(solution)/shard_map/convert_element_type | solution.py:80
  226.9 8.2 %concatenate.48 = bf16[2,8,8,8,768]{4,3,2,1,0:T(8,128)(2,1)} reshape(bf16[16,64,24,32]{3,2,1,0:T(8,128)(2,1)} %copy.25) | data formatting | bytes 3145728 | tf_op jit(solution)/shard_map/concatenate | solution.py:85
  241.2 6.2 fusion.43
  247.5 163.1 %all-reduce.5.cloned.1.call-done = (f32[768,2304]{1,0:T(8,128)}, f32[768,768]{1,0:T(8,128)}) async-done(((f32[768,2304]{1,0:T(8,128)}, f32[768,768]{1,0:T(8,128)}), (f32[768,2304]{1,0:T(8,128)}, f32[768,768]{1,0:T(8,128)})) %all-reduce.5.cloned.1.call-update) | async-done | bytes 9437200 | tf_op jit(solution)/shard_map/psum | solution.py:158
  410.7 3.3 convolution_convert_fusion.2
  414.1 6.1 fusion.39
  422.9 4.9 collective-permute-done.8
  429.1 5.3 collective-permute-done.5
  436.3 15.3 %collective-permute-done.9 = bf16[4,64,768]{2,1,0:T(8,128)(2,1)S(1)} collective-permute-done((bf16[4,64,768]{2,1,0:T(8,128)(2,1)S(1)}, bf16[4,64,768]{2,1,0:T(8,128)(2,1)S(1)}, u32[]{:S(2)}, u32[]{:S(2)}) %collective-permute-start.9) | collective-permute-done | bytes 393248 | tf_op jit(solution)/shard_map/ppermute | solution.py:16
  453.5 182.1 %all-reduce.7.cloned.1.call-done = (f32[768,2304]{1,0:T(8,128)}, f32[768,768]{1,0:T(8,128)}) async-done(((f32[768,2304]{1,0:T(8,128)}, f32[768,768]{1,0:T(8,128)}), (f32[768,2304]{1,0:T(8,128)}, f32[768,768]{1,0:T(8,128)})) %all-reduce.7.cloned.1.call-update) | async-done | bytes 9437200 | tf_op jit(solution)/shard_map/psum | solution.py:158
  635.6 6.6 %copy.44 = f32[768,2304]{1,0:T(8,128)} copy(f32[768,2304]{1,0:T(8,128)} %get-tuple-element.20) | data formatting | bytes 14155776
  (115 shorter events, 60.1 us)
Async XLA Ops:
  7.2 48.3 %copy-start = (bf16[768,2304]{1,0:T(8,128)(2,1)S(1)}, bf16[768,2304]{1,0:T(8,128)(2,1)}, u32[]{:S(2)}) copy-start(bf16[768,2304]{1,0:T(8,128)(2,1)} %param.8) | copy-start | bytes 10616836
  7.2 403.4 %all-reduce.5.cloned.1.call-start = ((), (), s32[]{:S(2)}) async-start(), calls=%async_computation | async-start | bytes 18874368 | tf_op jit(solution)/shard_map/psum | solution.py:158
  7.2 13.0 %copy-start.9 = (bf16[16,64,768]{2,1,0:T(8,128)(2,1)S(1)}, bf16[16,64,768]{2,1,0:T(8,128)(2,1)}, u32[]{:S(2)}) copy-start(bf16[16,64,768]{2,1,0:T(8,128)(2,1)} %param.7) | copy-start | bytes 4718596
  8.1 13.2 %collective-permute-start.2 = (bf16[4,64]{1,0:T(4,128)(2,1)S(1)}, bf16[4,64]{1,0:T(4,128)(2,1)S(1)}, u32[]{:S(2)}, u32[]{:S(2)}) collective-permute-start(bf16[4,64]{1,0:T(4,128)(2,1)S(1)} %slice.99), channel_id=1, source_target_pairs={{1,0},{2,1},{3,2},{4,3},{5,4},{6,5},{7,6},{0,7},{9,8},{10,9},{11,1... | collective-permute-start | bytes 1544 | tf_op jit(solution)/shard_map/ppermute | solution.py:16
  14.5 21.3 %collective-permute-start.6 = (bf16[4,64,768]{2,1,0:T(8,128)(2,1)}, bf16[4,64,768]{2,1,0:T(8,128)(2,1)}, u32[]{:S(2)}, u32[]{:S(2)}) collective-permute-start(bf16[4,64,768]{2,1,0:T(8,128)(2,1)} %slice.88), channel_id=1, source_target_pairs={{1,0},{2,1},{3,2},{4,3},{5,4},{6,5},{7,6},{0,7},{9,8},{10,9},{11,1... | collective-permute-start | bytes 1179656 | tf_op jit(solution)/shard_map/ppermute | solution.py:16
  16.9 16.0 %collective-permute-start = (bf16[4,64,768]{2,1,0:T(8,128)(2,1)}, bf16[4,64,768]{2,1,0:T(8,128)(2,1)}, u32[]{:S(2)}, u32[]{:S(2)}) collective-permute-start(bf16[4,64,768]{2,1,0:T(8,128)(2,1)} %slice.73), channel_id=1, source_target_pairs={{1,0},{2,1},{3,2},{4,3},{5,4},{6,5},{7,6},{0,7},{9,8},{10,9},{11,1... | collective-permute-start | bytes 1179656 | tf_op jit(solution)/shard_map/ppermute | solution.py:16
  21.3 4.4 collective-permute-start.3
  28.6 13.1 %copy-start.7 = (bf16[12,64,768]{2,1,0:T(8,128)(2,1)S(1)}, bf16[12,64,768]{2,1,0:T(8,128)(2,1)}, u32[]{:S(2)}) copy-start(bf16[12,64,768]{2,1,0:T(8,128)(2,1)} %slice.72) | copy-start | bytes 3538948
  30.3 12.9 %copy-start.6 = (bf16[12,64,768]{2,1,0:T(8,128)(2,1)S(1)}, bf16[12,64,768]{2,1,0:T(8,128)(2,1)}, u32[]{:S(2)}) copy-start(bf16[12,64,768]{2,1,0:T(8,128)(2,1)} %slice.87) | copy-start | bytes 3538948
  33.9 12.1 %collective-permute-start.1 = (bf16[16,4,768]{2,1,0:T(4,128)(2,1)S(1)}, bf16[16,4,768]{2,1,0:T(4,128)(2,1)S(1)}, u32[]{:S(2)}, u32[]{:S(2)}) collective-permute-start(bf16[16,4,768]{2,1,0:T(4,128)(2,1)S(1)} %pad_maximum_fusion.7), channel_id=1, source_target_pairs={{8,0},{16,8},{24,16},{32,24},{40,32},{48,40},{56,48},{64,56},{72,6... | collective-permute-start | bytes 294920 | tf_op jit(solution)/shard_map/ppermute | solution.py:16
  37.5 11.2 %collective-permute-start.7 = (bf16[16,4,768]{2,1,0:T(4,128)(2,1)}, bf16[16,4,768]{2,1,0:T(4,128)(2,1)}, u32[]{:S(2)}, u32[]{:S(2)}) collective-permute-start(bf16[16,4,768]{2,1,0:T(4,128)(2,1)} %pad_maximum_fusion.6), channel_id=1, source_target_pairs={{8,0},{16,8},{24,16},{32,24},{40,32},{48,40},{56,48},{64,56},{72,6... | collective-permute-start | bytes 294920 | tf_op jit(solution)/shard_map/ppermute | solution.py:16
  43.2 4.1 copy-start.1
  48.6 2.9 copy-start.24
  53.0 2.0 copy-start.2
  53.0 2.0 copy-start.13
  53.0 2.0 copy-start.20
  150.0 10.7 %copy-start.5 = (bf16[16,64,768]{1,2,0:T(8,128)(2,1)S(1)}, bf16[16,64,768]{1,2,0:T(8,128)(2,1)}, u32[]{:S(2)}) copy-start(bf16[16,64,768]{1,2,0:T(8,128)(2,1)} %copy.15) | copy-start | bytes 4718596
  150.0 10.7 %copy-start.25 = (f32[16,24,64]{2,1,0:T(8,128)S(1)}, f32[16,24,64]{2,1,0:T(8,128)}, u32[]{:S(2)}) copy-start(f32[16,24,64]{2,1,0:T(8,128)} %get-tuple-element.13) | copy-start | bytes 294916
  184.1 2.8 copy-start.19
  239.1 2.1 copy-start.11
  247.4 388.1 %all-reduce.7.cloned.1.call-start = ((), (), s32[]{:S(2)}) async-start(), calls=%async_computation.1 | async-start | bytes 18874368 | tf_op jit(solution)/shard_map/psum | solution.py:158
  410.6 3.4 copy-start.4
  410.6 3.4 copy-start.15
  410.6 3.4 copy-start.21
  410.6 3.4 copy-start.23
  414.0 6.3 collective-permute-start.4
  420.4 14.1 %collective-permute-start.5 = (bf16[4,64,768]{2,1,0:T(8,128)(2,1)S(1)}, bf16[4,64,768]{2,1,0:T(8,128)(2,1)S(1)}, u32[]{:S(2)}, u32[]{:S(2)}) collective-permute-start(bf16[4,64,768]{2,1,0:T(8,128)(2,1)S(1)} %pad_maximum_fusion.5), channel_id=1, source_target_pairs={{7,0},{0,1},{1,2},{2,3},{3,4},{4,5},{5,6},{6,7},{15,8},{8,9},{9,10... | collective-permute-start | bytes 1179656 | tf_op jit(solution)/shard_map/ppermute | solution.py:16
  421.6 12.8 %copy-start.8 = (bf16[16,64,768]{2,1,0:T(8,128)(2,1)S(1)}, bf16[16,64,768]{2,1,0:T(8,128)(2,1)}, u32[]{:S(2)}) copy-start(bf16[16,64,768]{2,1,0:T(8,128)(2,1)} %param.5) | copy-start | bytes 4718596
  422.8 4.9 collective-permute-start.8
  427.7 23.9 %copy-start.10 = (bf16[16,64,768]{2,1,0:T(8,128)(2,1)S(1)}, bf16[16,64,768]{2,1,0:T(8,128)(2,1)}, u32[]{:S(2)}) copy-start(bf16[16,64,768]{2,1,0:T(8,128)(2,1)} %param.7) | copy-start | bytes 4718596
  427.8 23.8 %collective-permute-start.9 = (bf16[4,64,768]{2,1,0:T(8,128)(2,1)S(1)}, bf16[4,64,768]{2,1,0:T(8,128)(2,1)S(1)}, u32[]{:S(2)}, u32[]{:S(2)}) collective-permute-start(bf16[4,64,768]{2,1,0:T(8,128)(2,1)S(1)} %pad_maximum_fusion.4), channel_id=1, source_target_pairs={{7,0},{0,1},{1,2},{2,3},{3,4},{4,5},{5,6},{6,7},{15,8},{8,9},{9,10... | collective-permute-start | bytes 1179656 | tf_op jit(solution)/shard_map/ppermute | solution.py:16
  635.6 6.6 %copy-start.16 = (f32[768,768]{1,0:T(8,128)S(1)}, f32[768,768]{1,0:T(8,128)}, u32[]{:S(2)}) copy-start(f32[768,768]{1,0:T(8,128)} %get-tuple-element.21) | copy-start | bytes 7077892
  (6 other events, 7.8 us)
Sparse Core Ops, SparseCore 0:
  247.6 162.9 all-reduce.4
  413.2 222.3 all-reduce.6
